TPU v7x, 256 devices: a whole 4x4x8 slice. The times are simulated.
256 devices in a mesh: row: 16 (over z, core), col: 16 (over y, x).
Axes of the slice: x: 4, y: 4, z: 8, core: 2. Of those that a mesh axis runs over, the one named last changes fastest.
Arguments:
- clean_in: bfloat16 [512, 8192], P('row', 'col'), may hold values from -6 to 6
- corrupt_in: bfloat16 [512, 8192], P('row', 'col'), may hold values from -6 to 6
- patch_mask: int32 [512], replicated, may hold values 0 or 1
- gate_weight: bfloat16 [8192, 28672], P('col', 'row'), may hold values from -0.0625 to 0.0625
- up_weight: bfloat16 [8192, 28672], P('col', 'row'), may hold values from -0.0625 to 0.0625
- down_weight: bfloat16 [28672, 8192], P('row', 'col'), may hold values from -0.03125 to 0.03125
Outputs:
- clean_out: float32 [512, 8192], P('row', 'col')
- patched_out: float32 [512, 8192], P('row', 'col')
All inputs are finite; a program needn't handle non-finite values.
Results may differ from a plain program's by a relative error of at most 0.0029.
Values may be sent and summed in bfloat16 or wider, within the bound.
A program may use at most 128 MiB of HBM per device.

v0:
```python
import jax
import jax.numpy as jnp
from jax import lax
from jax.sharding import PartitionSpec as P


def on_device(clean_in, corrupt_in, patch_mask, gate_weight, up_weight, down_weight):
    stacked = jnp.stack((clean_in, corrupt_in), axis=1)
    piece = lax.all_gather(stacked, "row", axis=0, tiled=True)
    gate_part = jnp.einsum("tkd,df->tkf", piece, gate_weight, preferred_element_type=jnp.float32)
    up_part = jnp.einsum("tkd,df->tkf", piece, up_weight, preferred_element_type=jnp.float32)
    partial_sums = jnp.stack((gate_part, up_part), axis=2)
    summed = lax.psum_scatter(partial_sums, "col", scatter_dimension=0, tiled=True)
    row_count = summed.shape[0]
    row_mask = lax.dynamic_slice_in_dim(patch_mask, lax.axis_index("col") * row_count, row_count, 0)
    hidden = (jax.nn.silu(summed[:, :, 0]) * summed[:, :, 1]).astype(jnp.bfloat16)
    patched = jnp.where(row_mask[:, None] == 1, hidden[:, 0], hidden[:, 1])
    paired = jnp.stack((hidden[:, 0], patched), axis=1)
    gathered = lax.all_gather(paired, "col", axis=0, tiled=True)
    result = lax.psum_scatter(
        jnp.einsum("tkf,fd->tkd", gathered, down_weight, preferred_element_type=jnp.float32),
        "row",
        scatter_dimension=0,
        tiled=True,
    )
    return (result[:, 0], result[:, 1])


def solution(mesh):
    placed = (
        P("row", "col"),
        P("row", "col"),
        P(),
        P("col", "row"),
        P("col", "row"),
        P("row", "col"),
    )
    return jax.shard_map(
        on_device,
        mesh=mesh,
        in_specs=placed,
        out_specs=(P("row", "col"), P("row", "col")),
        check_vma=False,
    )
```

profile of v0, /device:TPU:2, one launch (start us, length us, event | category | flops | bytes accessed | tf_op | source)
XLA Modules:
  0.0 311.0 jit_solution(6040133685950640488)
XLA Ops:
  7.2 0.0 copy-start
  7.2 0.0 all-gather.3.cloned.1.call-start
  7.2 1.5 pad_maximum_fusion.2
  8.8 0.0 all-gather.3.cloned.1.call-update
  8.8 0.0 reduce-scatter.3.cloned.1.call-start
  8.8 43.1 %all-gather.3.cloned.1.call-done = bf16[512,2,512]{2,0,1:T(8,128)(2,1)} async-done(((bf16[32,2,512]{2,0,1:T(8,128)(2,1)}), bf16[512,2,512]{2,0,1:T(8,128)(2,1)}) %all-gather.3.cloned.1.call-update) | async-done | bytes 1048592 | tf_op jit(solution)/shard_map/all_gather | solution.py:9
  52.0 0.0 copy-done
  52.0 0.0 copy-start.1
  52.0 0.0 copy-start.2
  52.0 6.4 %convolution_bitcast_fusion = f32[512,2,1,1792]{3,0,1,2:T(8,128)} fusion(bf16[512,2,512]{2,0,1:T(8,128)(2,1)} %all-gather.3.cloned.1.call-done, bf16[512,1792]{1,0:T(8,128)(2,1)S(1)} %copy-done), kind=kOutput, calls=%fused_computation.1 | convolution fusion | flops 1879048192 | bytes 10223616 | tf_op jit(solution)/shard_map/tkd,df->tkf/dot_general | solution.py:11
  58.3 0.0 copy-done.1
  58.3 0.0 copy-done.2
  58.3 5.0 %convolution_bitcast_fusion.1 = f32[512,2,1,1792]{3,0,1,2:T(8,128)} fusion(bf16[512,2,512]{2,0,1:T(8,128)(2,1)S(1)} %copy-done.2, bf16[512,1792]{1,0:T(8,128)(2,1)S(1)} %copy-done.1), kind=kOutput, calls=%fused_computation.2 | convolution fusion | flops 1879048192 | bytes 10223616 | tf_op jit(solution)/shard_map/tkd,df->tkf/dot_general | solution.py:10
  63.4 11.9 %pad_maximum_fusion = f32[512,2,2,1792]{3,0,1,2:T(8,128)} fusion(f32[512,2,1,1792]{3,0,1,2:T(8,128)} %convolution_bitcast_fusion, f32[512,2,1,1792]{3,0,1,2:T(8,128)} %convolution_bitcast_fusion.1), kind=kLoop, calls=%fused_computation | loop fusion | flops 3670016 | bytes 29360128 | tf_op jit(solution)/shard_map/stack | solution.py:12
  75.3 0.0 reduce-scatter.3.cloned.1.call-update
  75.3 0.0 all-gather.5.cloned.1.call-start
  75.3 0.8 dynamic-slice_compare_fusion
  76.1 104.8 %reduce-scatter.3.cloned.1.call-done = f32[32,2,2,1792]{3,0,1,2:T(8,128)} async-done(((f32[512,2,2,1792]{3,0,1,2:T(8,128)}), f32[32,2,2,1792]{3,0,1,2:T(8,128)}) %reduce-scatter.3.cloned.1.call-update) | async-done | bytes 917520 | tf_op jit(solution)/shard_map/reduce_scatter | solution.py:13
  180.9 1.3 fusion.5
  182.2 0.1 fusion.6
  182.3 0.7 pad_maximum_fusion.1
  183.0 0.0 all-gather.5.cloned.1.call-update
  183.0 0.0 reduce-scatter.5.cloned.1.call-start
  183.1 54.0 %all-gather.5.cloned.1.call-done = bf16[512,2,1792]{2,0,1:T(8,128)(2,1)} async-done(((bf16[32,2,1792]{2,0,1:T(8,128)(2,1)}), bf16[512,2,1792]{2,0,1:T(8,128)(2,1)}) %all-gather.5.cloned.1.call-update) | async-done | bytes 3670032 | tf_op jit(solution)/shard_map/all_gather | solution.py:19
  237.0 6.0 %fusion = f32[512,2,512]{2,0,1:T(8,128)} fusion(bf16[512,2,1792]{2,0,1:T(8,128)(2,1)} %all-gather.5.cloned.1.call-done, bf16[1792,512]{1,0:T(8,128)(2,1)} %param.11), kind=kOutput, calls=%fused_computation.3 | convolution fusion | flops 1879048192 | bytes 7602176 | tf_op jit(solution)/shard_map/tkf,fd->tkd/dot_general | solution.py:21
  243.0 0.0 reduce-scatter.5.cloned.1.call-update
  243.1 59.8 %reduce-scatter.5.cloned.1.call-done = f32[32,2,512]{2,0,1:T(8,128)} async-done(((f32[512,2,512]{2,0,1:T(8,128)}), f32[32,2,512]{2,0,1:T(8,128)}) %reduce-scatter.5.cloned.1.call-update) | async-done | bytes 131088 | tf_op jit(solution)/shard_map/reduce_scatter | solution.py:20
  302.9 1.5 slice_bitcast_fusion.2
Async XLA Ops:
  7.2 44.8 %copy-start = (bf16[512,1792]{1,0:T(8,128)(2,1)S(1)}, bf16[512,1792]{1,0:T(8,128)(2,1)}, u32[]{:S(2)}) copy-start(bf16[512,1792]{1,0:T(8,128)(2,1)} %param.10) | copy-start | bytes 5505028
  7.2 44.8 %all-gather.3.cloned.1.call-start = ((), (), s32[]{:S(2)}) async-start(), calls=%async_computation.2 | async-start | bytes 1114112 | tf_op jit(solution)/shard_map/all_gather | solution.py:9
  8.8 172.1 %reduce-scatter.3.cloned.1.call-start = ((), (), s32[]{:S(2)}) async-start(), calls=%async_computation.3 | async-start | bytes 15597568 | tf_op jit(solution)/shard_map/reduce_scatter | solution.py:13
  52.0 6.4 %copy-start.1 = (bf16[512,1792]{1,0:T(8,128)(2,1)S(1)}, bf16[512,1792]{1,0:T(8,128)(2,1)}, u32[]{:S(2)}) copy-start(bf16[512,1792]{1,0:T(8,128)(2,1)} %param.9) | copy-start | bytes 5505028
  52.0 6.4 %copy-start.2 = (bf16[512,2,512]{2,0,1:T(8,128)(2,1)S(1)}, bf16[512,2,512]{2,0,1:T(8,128)(2,1)}, u32[]{:S(2)}) copy-start(bf16[512,2,512]{2,0,1:T(8,128)(2,1)} %all-gather.3.cloned.1.call-done) | copy-start | bytes 3145732
  75.3 161.8 %all-gather.5.cloned.1.call-start = ((), (), s32[]{:S(2)}) async-start(), calls=%async_computation.4 | async-start | bytes 3899392 | tf_op jit(solution)/shard_map/all_gather | solution.py:19
  183.0 119.9 %reduce-scatter.5.cloned.1.call-start = ((), (), s32[]{:S(2)}) async-start(), calls=%async_computation.5 | async-start | bytes 2228224 | tf_op jit(solution)/shard_map/reduce_scatter | solution.py:20
Sparse Core Ops, SparseCore 0:
  10.4 41.5 all-gather.2
  75.4 105.4 reduce-scatter.2
  183.3 53.6 all-gather.4
  243.2 59.6 reduce-scatter.4
where the time goes:
time: 311 us
  waiting for transfers between devices  262 us (84%)
  matrix products  17.4 us (6%)
  other arithmetic  16.3 us (5%)
  between operations  13.8 us (4%)
    reduce_scatter x1, waiting for transfers between devices, on_device(): lax.psum_scatter(partial_sums, 'col', scatter_dimension=0, tiled=True)  105 us
    reduce_scatter x1, waiting for transfers between devices, on_device(): lax.psum_scatter(jnp.einsum('tkf,fd->tkd', gathered, down_weight, preferr...  59.8 us
    all_gather x1, waiting for transfers between devices, on_device(): gathered = lax.all_gather(paired, 'col', axis=0, tiled=True)  54 us
    all_gather x1, waiting for transfers between devices, on_device(): piece = lax.all_gather(stacked, 'row', axis=0, tiled=True)  43.1 us
    another operation x1, other arithmetic, on_device(): partial_sums = jnp.stack((gate_part, up_part), axis=2)  11.9 us
    dot_general x1, matrix products, on_device(): jnp.einsum('tkd,df->tkf', piece, up_weight, preferred_element_type=jnp.fl...  6.36 us
  transfers between devices with their start and end apart: 4, of which 4 were waited for; matrix products, arithmetic and copies ran while one was open for 0% of the time, Pallas kernels for 0%

commit v1 on v0

--- a/solution.py
+++ b/solution.py
@@ -4,9 +4,27 @@
 from jax.sharding import PartitionSpec as P
 
 
+def collect(value, axis, dim):
+    ways, here, lap = (lax.axis_size(axis), lax.axis_index(axis), value.shape[dim])
+    shape = [n * ways if d == dim else n for d, n in enumerate(value.shape)]
+    full = lax.dynamic_update_slice_in_dim(
+        jnp.zeros(shape, value.dtype), value, here * lap, axis=dim
+    )
+    going_up = going_down = value
+    for far in range(1, ways // 2 + 1):
+        going_up = lax.ppermute(going_up, axis, [(d, (d + 1) % ways) for d in range(ways)])
+        full = lax.dynamic_update_slice_in_dim(full, going_up, (here - far) % ways * lap, axis=dim)
+        if 2 * far < ways:
+            going_down = lax.ppermute(going_down, axis, [(d, (d - 1) % ways) for d in range(ways)])
+            full = lax.dynamic_update_slice_in_dim(
+                full, going_down, (here + far) % ways * lap, axis=dim
+            )
+    return full
+
+
 def on_device(clean_in, corrupt_in, patch_mask, gate_weight, up_weight, down_weight):
     stacked = jnp.stack((clean_in, corrupt_in), axis=1)
-    piece = lax.all_gather(stacked, "row", axis=0, tiled=True)
+    piece = collect(stacked, "row", 0)
     gate_part = jnp.einsum("tkd,df->tkf", piece, gate_weight, preferred_element_type=jnp.float32)
     up_part = jnp.einsum("tkd,df->tkf", piece, up_weight, preferred_element_type=jnp.float32)
     partial_sums = jnp.stack((gate_part, up_part), axis=2)

time: 311 us -> 310 us (level)
  starting transfers between devices: 0.16 us -> 23.3 us
  waiting for transfers between devices: 262 us -> 239 us
    all_gather x1 -> x0, waiting for transfers between devices: 43.1 us -> none  [on_device(): piece = lax.all_gather(stacked, 'row', axis=0, tiled=True)]
    ppermute x0 -> x15, starting transfers between devices: none -> 23.2 us  [the longest x7 23.1 us: collect(): lax.ppermute(going_down, axis, [(d, (d - 1) % ways) for d in range(ways)])]
    ppermute x0 -> x15, waiting for transfers between devices: none -> 18.2 us  [the longest x8 18.1 us: collect(): lax.ppermute(going_up, axis, [(d, (d + 1) % ways) for d in range(ways)])]
  transfers between devices with their start and end apart: 4 -> 18, of which waited for: 4 -> 11; matrix products, arithmetic and copies ran while one was open for 0% -> 0% of each run, Pallas kernels for 0% -> 0%
where the time goes in v1:
time: 310 us; the launch traced here: 309 us
  waiting for transfers between devices  239 us (77%)
  starting transfers between devices  23.3 us (8%)
  matrix products  16 us (5%)
  other arithmetic  15.7 us (5%)
  between operations  13.9 us (4%)
    reduce_scatter x1, waiting for transfers between devices, on_device(): lax.psum_scatter(partial_sums, 'col', scatter_dimension=0, tiled=True)  107 us
    reduce_scatter x1, waiting for transfers between devices, on_device(): lax.psum_scatter(jnp.einsum('tkf,fd->tkd', gathered, down_weight, preferr...  59.8 us
    all_gather x1, waiting for transfers between devices, on_device(): gathered = lax.all_gather(paired, 'col', axis=0, tiled=True)  54 us
    ppermute x7, starting transfers between devices, collect(): lax.ppermute(going_down, axis, [(d, (d - 1) % ways) for d in range(ways)])  23.1 us
    ppermute x8, waiting for transfers between devices, collect(): lax.ppermute(going_up, axis, [(d, (d + 1) % ways) for d in range(ways)])  18.1 us
    another operation x1, other arithmetic, on_device(): partial_sums = jnp.stack((gate_part, up_part), axis=2)  11.9 us
  transfers between devices with their start and end apart: 18, of which 11 were waited for; matrix products, arithmetic and copies ran while one was open for 0% of the time, Pallas kernels for 0%

profile of v1, /device:TPU:2, one launch (start us, length us, event | category | flops | bytes accessed | tf_op | source)
XLA Modules:
  0.0 309.3 jit_solution(6225265835234675924)
XLA Ops:
  7.2 0.0 copy-start
  7.2 0.0 reduce-scatter.3.cloned.1.call-start
  7.2 0.1 broadcast_in_dim.12
  7.3 0.9 pad_maximum_fusion.2
  8.2 0.0 collective-permute-start
  8.2 5.3 %collective-permute-start.1 = (bf16[32,2,512]{2,0,1:T(8,128)(2,1)S(1)}, bf16[32,2,512]{2,0,1:T(8,128)(2,1)S(1)}, u32[]{:S(2)}, u32[]{:S(2)}) collective-permute-start(bf16[32,2,512]{2,0,1:T(8,128)(2,1)S(1)} %get-tuple-element.6), channel_id=1, source_target_pairs={{0,240},{16,0},{32,16},{48,32},{64,48},{80,64},{96,80},{112,96},{1... | collective-permute-start | bytes 196616 | tf_op jit(solution)/shard_map/ppermute | solution.py:18
  13.5 1.9 collective-permute-done
  15.5 0.0 collective-permute-start.2
  15.5 0.0 collective-permute-done.1
  15.5 3.0 collective-permute-start.3
  18.5 1.9 collective-permute-done.2
  20.4 0.0 collective-permute-start.4
  20.4 0.0 collective-permute-done.3
  20.4 3.0 collective-permute-start.5
  23.4 1.9 collective-permute-done.4
  25.3 0.0 collective-permute-start.6
  25.3 0.0 collective-permute-done.5
  25.3 3.0 collective-permute-start.7
  28.3 1.9 collective-permute-done.6
  30.2 0.0 collective-permute-start.8
  30.2 0.0 collective-permute-done.7
  30.2 3.0 collective-permute-start.9
  33.2 1.9 collective-permute-done.8
  35.1 0.0 collective-permute-start.10
  35.1 0.0 collective-permute-done.9
  35.1 3.0 collective-permute-start.11
  38.1 1.9 collective-permute-done.10
  40.0 0.0 collective-permute-start.12
  40.0 0.0 collective-permute-done.11
  40.0 3.0 collective-permute-start.13
  43.0 1.9 collective-permute-done.12
  44.9 0.0 collective-permute-start.14
  44.9 0.0 collective-permute-done.13
  44.9 4.9 %collective-permute-done.14 = bf16[32,2,512]{2,0,1:T(8,128)(2,1)S(1)} collective-permute-done((bf16[32,2,512]{2,0,1:T(8,128)(2,1)S(1)}, bf16[32,2,512]{2,0,1:T(8,128)(2,1)S(1)}, u32[]{:S(2)}, u32[]{:S(2)}) %collective-permute-start.14) | collective-permute-done | bytes 65568 | tf_op jit(solution)/shard_map/ppermute | solution.py:15
  49.8 0.0 copy-done
  49.8 0.0 copy-start.1
  49.8 5.0 %convolution_bitcast_fusion = f32[512,2,1,1792]{3,0,1,2:T(8,128)} fusion(bf16[512,2,512]{2,0,1:T(8,128)(2,1)S(1)} %constant_dynamic-update-slice_fusion, bf16[512,1792]{1,0:T(8,128)(2,1)S(1)} %copy-done), kind=kOutput, calls=%fused_computation.1 | convolution fusion | flops 1879048192 | bytes 10223616 | tf_op jit(solution)/shard_map/tkd,df->tkf/dot_general | solution.py:29
  54.8 0.0 copy-done.1
  54.8 5.0 %convolution_bitcast_fusion.1 = f32[512,2,1,1792]{3,0,1,2:T(8,128)} fusion(bf16[512,2,512]{2,0,1:T(8,128)(2,1)S(1)} %constant_dynamic-update-slice_fusion, bf16[512,1792]{1,0:T(8,128)(2,1)S(1)} %copy-done.1), kind=kOutput, calls=%fused_computation.2 | convolution fusion | flops 1879048192 | bytes 10223616 | tf_op jit(solution)/shard_map/tkd,df->tkf/dot_general | solution.py:28
  59.8 11.9 %pad_maximum_fusion = f32[512,2,2,1792]{3,0,1,2:T(8,128)} fusion(f32[512,2,1,1792]{3,0,1,2:T(8,128)} %convolution_bitcast_fusion, f32[512,2,1,1792]{3,0,1,2:T(8,128)} %convolution_bitcast_fusion.1), kind=kLoop, calls=%fused_computation | loop fusion | flops 3670016 | bytes 29360128 | tf_op jit(solution)/shard_map/stack | solution.py:30
  71.8 0.0 reduce-scatter.3.cloned.1.call-update
  71.8 0.0 all-gather.2.cloned.1.call-start
  71.8 0.8 dynamic-slice_compare_fusion
  72.6 106.7 %reduce-scatter.3.cloned.1.call-done = f32[32,2,2,1792]{3,0,1,2:T(8,128)} async-done(((f32[512,2,2,1792]{3,0,1,2:T(8,128)}), f32[32,2,2,1792]{3,0,1,2:T(8,128)}) %reduce-scatter.3.cloned.1.call-update) | async-done | bytes 917520 | tf_op jit(solution)/shard_map/reduce_scatter | solution.py:31
  179.3 1.3 fusion.5
  180.6 0.1 fusion.6
  180.7 0.7 pad_maximum_fusion.1
  181.4 0.0 all-gather.2.cloned.1.call-update
  181.4 0.0 reduce-scatter.5.cloned.1.call-start
  181.4 54.0 %all-gather.2.cloned.1.call-done = bf16[512,2,1792]{2,0,1:T(8,128)(2,1)} async-done(((bf16[32,2,1792]{2,0,1:T(8,128)(2,1)}), bf16[512,2,1792]{2,0,1:T(8,128)(2,1)}) %all-gather.2.cloned.1.call-update) | async-done | bytes 3670032 | tf_op jit(solution)/shard_map/all_gather | solution.py:37
  235.4 6.0 %fusion = f32[512,2,512]{2,0,1:T(8,128)} fusion(bf16[512,2,1792]{2,0,1:T(8,128)(2,1)} %all-gather.2.cloned.1.call-done, bf16[1792,512]{1,0:T(8,128)(2,1)} %param.11), kind=kOutput, calls=%fused_computation.3 | convolution fusion | flops 1879048192 | bytes 7602176 | tf_op jit(solution)/shard_map/tkf,fd->tkd/dot_general | solution.py:39
  241.4 0.0 reduce-scatter.5.cloned.1.call-update
  241.4 59.8 %reduce-scatter.5.cloned.1.call-done = f32[32,2,512]{2,0,1:T(8,128)} async-done(((f32[512,2,512]{2,0,1:T(8,128)}), f32[32,2,512]{2,0,1:T(8,128)}) %reduce-scatter.5.cloned.1.call-update) | async-done | bytes 131088 | tf_op jit(solution)/shard_map/reduce_scatter | solution.py:38
  301.3 1.5 slice_bitcast_fusion.2
  (15 shorter events, 0.1 us)
Async XLA Ops:
  7.2 42.6 %copy-start = (bf16[512,1792]{1,0:T(8,128)(2,1)S(1)}, bf16[512,1792]{1,0:T(8,128)(2,1)}, u32[]{:S(2)}) copy-start(bf16[512,1792]{1,0:T(8,128)(2,1)} %param.10) | copy-start | bytes 5505028
  7.2 172.1 %reduce-scatter.3.cloned.1.call-start = ((), (), s32[]{:S(2)}) async-start(), calls=%async_computation.2 | async-start | bytes 15597568 | tf_op jit(solution)/shard_map/reduce_scatter | solution.py:31
  8.2 7.3 %collective-permute-start = (bf16[32,2,512]{2,0,1:T(8,128)(2,1)S(1)}, bf16[32,2,512]{2,0,1:T(8,128)(2,1)S(1)}, u32[]{:S(2)}, u32[]{:S(2)}) collective-permute-start(bf16[32,2,512]{2,0,1:T(8,128)(2,1)S(1)} %get-tuple-element.6), channel_id=1, source_target_pairs={{0,16},{16,32},{32,48},{48,64},{64,80},{80,96},{96,112},{112,128},... | collective-permute-start | bytes 196616 | tf_op jit(solution)/shard_map/ppermute | solution.py:15
  8.2 7.2 %collective-permute-start.1 = (bf16[32,2,512]{2,0,1:T(8,128)(2,1)S(1)}, bf16[32,2,512]{2,0,1:T(8,128)(2,1)S(1)}, u32[]{:S(2)}, u32[]{:S(2)}) collective-permute-start(bf16[32,2,512]{2,0,1:T(8,128)(2,1)S(1)} %get-tuple-element.6), channel_id=1, source_target_pairs={{0,240},{16,0},{32,16},{48,32},{64,48},{80,64},{96,80},{112,96},{1... | collective-permute-start | bytes 196616 | tf_op jit(solution)/shard_map/ppermute | solution.py:18
  15.5 4.9 %collective-permute-start.2 = (bf16[32,2,512]{2,0,1:T(8,128)(2,1)S(1)}, bf16[32,2,512]{2,0,1:T(8,128)(2,1)S(1)}, u32[]{:S(2)}, u32[]{:S(2)}) collective-permute-start(bf16[32,2,512]{2,0,1:T(8,128)(2,1)S(1)} %collective-permute-done), channel_id=1, source_target_pairs={{0,16},{16,32},{32,48},{48,64},{64,80},{80,96},{96,112},{112,128},... | collective-permute-start | bytes 196616 | tf_op jit(solution)/shard_map/ppermute | solution.py:15
  15.5 4.9 %collective-permute-start.3 = (bf16[32,2,512]{2,0,1:T(8,128)(2,1)S(1)}, bf16[32,2,512]{2,0,1:T(8,128)(2,1)S(1)}, u32[]{:S(2)}, u32[]{:S(2)}) collective-permute-start(bf16[32,2,512]{2,0,1:T(8,128)(2,1)S(1)} %collective-permute-done.1), channel_id=1, source_target_pairs={{0,240},{16,0},{32,16},{48,32},{64,48},{80,64},{96,80},{112,96},{1... | collective-permute-start | bytes 196616 | tf_op jit(solution)/shard_map/ppermute | solution.py:18
  20.4 4.9 %collective-permute-start.4 = (bf16[32,2,512]{2,0,1:T(8,128)(2,1)S(1)}, bf16[32,2,512]{2,0,1:T(8,128)(2,1)S(1)}, u32[]{:S(2)}, u32[]{:S(2)}) collective-permute-start(bf16[32,2,512]{2,0,1:T(8,128)(2,1)S(1)} %collective-permute-done.2), channel_id=1, source_target_pairs={{0,16},{16,32},{32,48},{48,64},{64,80},{80,96},{96,112},{112,128},... | collective-permute-start | bytes 196616 | tf_op jit(solution)/shard_map/ppermute | solution.py:15
  20.4 4.9 %collective-permute-start.5 = (bf16[32,2,512]{2,0,1:T(8,128)(2,1)S(1)}, bf16[32,2,512]{2,0,1:T(8,128)(2,1)S(1)}, u32[]{:S(2)}, u32[]{:S(2)}) collective-permute-start(bf16[32,2,512]{2,0,1:T(8,128)(2,1)S(1)} %collective-permute-done.3), channel_id=1, source_target_pairs={{0,240},{16,0},{32,16},{48,32},{64,48},{80,64},{96,80},{112,96},{1... | collective-permute-start | bytes 196616 | tf_op jit(solution)/shard_map/ppermute | solution.py:18
  25.3 4.9 %collective-permute-start.6 = (bf16[32,2,512]{2,0,1:T(8,128)(2,1)S(1)}, bf16[32,2,512]{2,0,1:T(8,128)(2,1)S(1)}, u32[]{:S(2)}, u32[]{:S(2)}) collective-permute-start(bf16[32,2,512]{2,0,1:T(8,128)(2,1)S(1)} %collective-permute-done.4), channel_id=1, source_target_pairs={{0,16},{16,32},{32,48},{48,64},{64,80},{80,96},{96,112},{112,128},... | collective-permute-start | bytes 196616 | tf_op jit(solution)/shard_map/ppermute | solution.py:15
  25.3 4.9 %collective-permute-start.7 = (bf16[32,2,512]{2,0,1:T(8,128)(2,1)S(1)}, bf16[32,2,512]{2,0,1:T(8,128)(2,1)S(1)}, u32[]{:S(2)}, u32[]{:S(2)}) collective-permute-start(bf16[32,2,512]{2,0,1:T(8,128)(2,1)S(1)} %collective-permute-done.5), channel_id=1, source_target_pairs={{0,240},{16,0},{32,16},{48,32},{64,48},{80,64},{96,80},{112,96},{1... | collective-permute-start | bytes 196616 | tf_op jit(solution)/shard_map/ppermute | solution.py:18
  30.2 4.9 %collective-permute-start.8 = (bf16[32,2,512]{2,0,1:T(8,128)(2,1)S(1)}, bf16[32,2,512]{2,0,1:T(8,128)(2,1)S(1)}, u32[]{:S(2)}, u32[]{:S(2)}) collective-permute-start(bf16[32,2,512]{2,0,1:T(8,128)(2,1)S(1)} %collective-permute-done.6), channel_id=1, source_target_pairs={{0,16},{16,32},{32,48},{48,64},{64,80},{80,96},{96,112},{112,128},... | collective-permute-start | bytes 196616 | tf_op jit(solution)/shard_map/ppermute | solution.py:15
  30.2 4.9 %collective-permute-start.9 = (bf16[32,2,512]{2,0,1:T(8,128)(2,1)S(1)}, bf16[32,2,512]{2,0,1:T(8,128)(2,1)S(1)}, u32[]{:S(2)}, u32[]{:S(2)}) collective-permute-start(bf16[32,2,512]{2,0,1:T(8,128)(2,1)S(1)} %collective-permute-done.7), channel_id=1, source_target_pairs={{0,240},{16,0},{32,16},{48,32},{64,48},{80,64},{96,80},{112,96},{1... | collective-permute-start | bytes 196616 | tf_op jit(solution)/shard_map/ppermute | solution.py:18
  35.1 4.9 %collective-permute-start.10 = (bf16[32,2,512]{2,0,1:T(8,128)(2,1)S(1)}, bf16[32,2,512]{2,0,1:T(8,128)(2,1)S(1)}, u32[]{:S(2)}, u32[]{:S(2)}) collective-permute-start(bf16[32,2,512]{2,0,1:T(8,128)(2,1)S(1)} %collective-permute-done.8), channel_id=1, source_target_pairs={{0,16},{16,32},{32,48},{48,64},{64,80},{80,96},{96,112},{112,128},... | collective-permute-start | bytes 196616 | tf_op jit(solution)/shard_map/ppermute | solution.py:15
  35.1 4.9 %collective-permute-start.11 = (bf16[32,2,512]{2,0,1:T(8,128)(2,1)S(1)}, bf16[32,2,512]{2,0,1:T(8,128)(2,1)S(1)}, u32[]{:S(2)}, u32[]{:S(2)}) collective-permute-start(bf16[32,2,512]{2,0,1:T(8,128)(2,1)S(1)} %collective-permute-done.9), channel_id=1, source_target_pairs={{0,240},{16,0},{32,16},{48,32},{64,48},{80,64},{96,80},{112,96},{1... | collective-permute-start | bytes 196616 | tf_op jit(solution)/shard_map/ppermute | solution.py:18
  40.0 4.9 %collective-permute-start.12 = (bf16[32,2,512]{2,0,1:T(8,128)(2,1)S(1)}, bf16[32,2,512]{2,0,1:T(8,128)(2,1)S(1)}, u32[]{:S(2)}, u32[]{:S(2)}) collective-permute-start(bf16[32,2,512]{2,0,1:T(8,128)(2,1)S(1)} %collective-permute-done.10), channel_id=1, source_target_pairs={{0,16},{16,32},{32,48},{48,64},{64,80},{80,96},{96,112},{112,128},... | collective-permute-start | bytes 196616 | tf_op jit(solution)/shard_map/ppermute | solution.py:15
  40.0 4.9 %collective-permute-start.13 = (bf16[32,2,512]{2,0,1:T(8,128)(2,1)S(1)}, bf16[32,2,512]{2,0,1:T(8,128)(2,1)S(1)}, u32[]{:S(2)}, u32[]{:S(2)}) collective-permute-start(bf16[32,2,512]{2,0,1:T(8,128)(2,1)S(1)} %collective-permute-done.11), channel_id=1, source_target_pairs={{0,240},{16,0},{32,16},{48,32},{64,48},{80,64},{96,80},{112,96},{1... | collective-permute-start | bytes 196616 | tf_op jit(solution)/shard_map/ppermute | solution.py:18
  44.9 4.9 %collective-permute-start.14 = (bf16[32,2,512]{2,0,1:T(8,128)(2,1)S(1)}, bf16[32,2,512]{2,0,1:T(8,128)(2,1)S(1)}, u32[]{:S(2)}, u32[]{:S(2)}) collective-permute-start(bf16[32,2,512]{2,0,1:T(8,128)(2,1)S(1)} %collective-permute-done.12), channel_id=1, source_target_pairs={{0,16},{16,32},{32,48},{48,64},{64,80},{80,96},{96,112},{112,128},... | collective-permute-start | bytes 196616 | tf_op jit(solution)/shard_map/ppermute | solution.py:15
  49.8 5.0 %copy-start.1 = (bf16[512,1792]{1,0:T(8,128)(2,1)S(1)}, bf16[512,1792]{1,0:T(8,128)(2,1)}, u32[]{:S(2)}) copy-start(bf16[512,1792]{1,0:T(8,128)(2,1)} %param.9) | copy-start | bytes 5505028
  71.8 163.6 %all-gather.2.cloned.1.call-start = ((), (), s32[]{:S(2)}) async-start(), calls=%async_computation.3 | async-start | bytes 3899392 | tf_op jit(solution)/shard_map/all_gather | solution.py:37
  181.4 119.9 %reduce-scatter.5.cloned.1.call-start = ((), (), s32[]{:S(2)}) async-start(), calls=%async_computation.4 | async-start | bytes 2228224 | tf_op jit(solution)/shard_map/reduce_scatter | solution.py:38
Sparse Core Ops, SparseCore 0:
  71.9 107.3 reduce-scatter.2
  181.7 53.6 all-gather.1
  241.6 59.6 reduce-scatter.4
